TPU v7x, 128 devices: a whole 4x4x4 slice. The times are simulated.
128 devices in a mesh: row: 16 (over z, x), col: 8 (over y, core).
Axes of the slice: x: 4, y: 4, z: 4, core: 2. Of those that a mesh axis runs over, the one named last changes fastest.
Arguments:
- child_front: bfloat16 [16, 4096, 1024], P('row', 'col'), may hold values from -6 to 6
- child_inverse: bfloat16 [16, 1024, 1024], P('row'), as said below
- child_index: int32 [16, 32], P('row'), may hold values from 0 to 79, as said below
- child_size: int32 [16], P('row'), may hold values from 4 to 32, as said below
- front: float32 [10240, 10240], P('row', 'col'), may hold values from -6 to 6
- panel_inverse: float32 [256, 256], replicated, as said below
Outputs:
- trailing: float32 [10240, 10240], P('row', 'col')
- panel_rows: float32 [10240, 256], P('row')
Inputs may be any that keep to these rules, and one draw needn't show every extreme that they name: `child_index`: for each child r, the entries t < child_size[r] are increasing root tile numbers; later entries are arbitrary tile numbers and are not used. Cutting the root tiles into aligned runs of 5 tiles, a child has at most 2 live tiles in any run, and exactly 2 in each of two neighbouring runs 2q and 2q + 1 for some q. `child_size`: some child has the smallest and some child the largest possible size in every draw. `child_inverse`: lower triangular with a positive diagonal. `panel_inverse`: lower triangular with a positive diagonal.
All inputs are finite; a program needn't handle non-finite values.
Results may differ from a plain program's by a relative error of at most 0.0034.
Values may be sent and summed in bfloat16 or wider, within the bound.
A program may use at most 128 MiB of HBM per device.

v0:
```python
import jax
import jax.numpy as jnp
from jax import lax
from jax.sharding import PartitionSpec as P

TILE = 128
PANEL = 256
BLOCK_TILES = 2


def from_root(value, axis, source):
    kept = jnp.where(lax.axis_index(axis) == source, value, 0).astype(value.dtype)
    return lax.psum(kept, axis)


def slot_tiles(tile_index, first_slot, slot_count, slot_width, base_tile, sentinel):
    positions = jnp.arange(slot_width, dtype=jnp.int32)
    picked = jnp.take(tile_index, jnp.clip(first_slot + positions, 0, tile_index.shape[0] - 1))
    return jnp.where(positions < slot_count, picked - base_tile, sentinel)


def shards(child_front, child_inverse, child_index, child_size, front, panel_inverse):
    precise = lax.Precision.HIGHEST
    rows_dev = front.shape[0]
    cols_dev = front.shape[1]
    tiles_row = rows_dev // TILE
    tiles_col = cols_dev // TILE
    blocks = lax.axis_size("row")
    column = lax.axis_index("col")
    double = 2 * BLOCK_TILES
    factor_part = lax.dot_general(
        child_front[0],
        child_inverse[0],
        (((1,), (1,)), ((), ())),
        preferred_element_type=jnp.float32,
    ).astype(jnp.bfloat16)
    factor = lax.all_gather(factor_part, "col", axis=0, tiled=True)
    tile_index = child_index[0]
    live_tiles = jnp.arange(tile_index.shape[0], dtype=jnp.int32) < child_size[0]
    row_owner = jnp.where(live_tiles, tile_index // tiles_row, blocks)
    targets = jnp.arange(blocks, dtype=jnp.int32)
    starts = jnp.sum((row_owner[None, :] < targets[:, None]).astype(jnp.int32), axis=1)
    counts = jnp.sum((row_owner[None, :] == targets[:, None]).astype(jnp.int32), axis=1)
    col_owner = jnp.where(live_tiles, tile_index // tiles_col, lax.axis_size("col"))
    col_start = jnp.sum((col_owner < column).astype(jnp.int32))
    col_count = jnp.sum((col_owner == column).astype(jnp.int32))
    padded = jnp.concatenate(
        [factor, jnp.zeros((double * TILE, factor.shape[1]), factor.dtype)], axis=0
    )

    def row_rows(first_tile):
        return lax.dynamic_slice_in_dim(padded, first_tile * TILE, BLOCK_TILES * TILE, 0)

    def row_slots(first_tile, tile_count, target):
        return slot_tiles(
            tile_index, first_tile, tile_count, BLOCK_TILES, target * tiles_row, tiles_row
        )

    row_parts = jax.vmap(row_rows)(starts)
    col_part = lax.dynamic_slice_in_dim(padded, col_start * TILE, double * TILE, 0)
    row_targets = jax.vmap(row_slots)(starts, counts, targets)
    col_targets = slot_tiles(
        tile_index, col_start, col_count, double, column * tiles_col, tiles_col
    )
    col_sent = jnp.broadcast_to(col_targets[None, :], (blocks, double))
    width = padded.shape[1]
    row_tiles = row_parts.reshape(blocks, BLOCK_TILES, TILE, width)
    col_tiles = col_part.reshape(double, TILE, width)
    contribution = -jnp.einsum(
        "ikap,jbp->ikjab", row_tiles, col_tiles, preferred_element_type=jnp.float32
    )
    arrived, arrived_rows, arrived_cols = (
        lax.all_to_all(contribution, "row", split_axis=0, concat_axis=0, tiled=True),
        lax.all_to_all(row_targets, "row", split_axis=0, concat_axis=0, tiled=True),
        lax.all_to_all(col_sent, "row", split_axis=0, concat_axis=0, tiled=True),
    )
    tiled = front.reshape(tiles_row, TILE, tiles_col, TILE)
    tiled = tiled.at[arrived_rows[:, :, None], :, arrived_cols[:, None, :], :].add(
        arrived, mode="drop"
    )
    assembled = tiled.reshape(rows_dev, cols_dev)
    own_panel = lax.dot_general(
        assembled[:, :PANEL], panel_inverse, (((1,), (1,)), ((), ())), precision=precise
    )
    panel_rows = from_root(own_panel, "col", 0)
    whole_panel = lax.all_gather(panel_rows, "row", axis=0, tiled=True)
    across = lax.dynamic_slice_in_dim(whole_panel, column * cols_dev, cols_dev, 0)
    trailing = assembled - lax.dot_general(
        panel_rows, across, (((1,), (1,)), ((), ())), precision=precise
    )
    return (trailing, panel_rows)


def solution(mesh):
    in_specs = (
        P("row", "col", None),
        P("row", None, None),
        P("row", None),
        P("row"),
        P("row", "col"),
        P(),
    )
    out_specs = (P("row", "col"), P("row", None))
    return jax.shard_map(shards, mesh=mesh, in_specs=in_specs, out_specs=out_specs, check_vma=False)
```

profile of v0, /device:TPU:1, one launch (start us, length us, event | category | flops | bytes accessed | tf_op | source)
XLA Modules:
  0.0 468.3 jit_solution(3586415045492164564)
XLA Ops:
  7.2 1.5 copy-done
  8.8 3.5 fusion.2
  13.2 0.7 gather_fusion
  14.0 0.7 subtract_select_fusion
  14.7 8.4 %all-to-all-start = ((s32[16,1,2]{2,1,0:T(1,128)}), s32[16,1,2]{2,1,0:T(1,128)S(1)}, u32[]{:S(2)}, u32[]{:S(2)}) async-start(s32[16,1,2]{2,1,0:T(1,128)} %bitcast.3), calls=%async_computation | async-start | bytes 16384 | tf_op jit(solution)/shard_map/all_to_all | solution.py:74
  23.2 0.7 fusion.12
  23.9 0.6 fusion.14
  24.5 0.6 gather_fusion.1
  25.8 1.3 compare_select_fusion.7
  27.2 38.6 %all-gather.3.cloned.1.call-done = bf16[4096,1024]{1,0:T(8,128)(2,1)} async-done(((bf16[512,1024]{1,0:T(8,128)(2,1)}), bf16[4096,1024]{1,0:T(8,128)(2,1)}) %all-gather.3.cloned.1.call-update) | async-done | bytes 8388624 | tf_op jit(solution)/shard_map/all_gather | solution.py:37
  65.7 8.0 %concatenate.10 = bf16[4608,1024]{1,0:T(8,128)(2,1)} pad(bf16[4096,1024]{1,0:T(8,128)(2,1)} %all-gather.3.cloned.1.call-done, bf16[]{:T(256)} %constant.41.clone.1), padding=0_512x0_0 | pad | bytes 17825794 | tf_op jit(solution)/shard_map/concatenate | solution.py:47
  73.7 51.5 %while.1 = (s32[]{:T(128)}, bf16[4608,1024]{1,0:T(8,128)(2,1)}, s32[16,2]{0,1:T(2,128)S(1)}, bf16[16,256,1024]{2,1,0:T(8,128)(2,1)}, s32[]{:T(128)}) while((s32[]{:T(128)}, bf16[4608,1024]{1,0:T(8,128)(2,1)}, s32[16,2]{0,1:T(2,128)S(1)}, bf16[16,256,1024]{2,1,0:T(8,128)(2,1)}, s32[]{:T(128)}) %tuple.22), condition=%wide.while_cond, body=%wide.while_body.sunk | while | flops 2 | bytes 1049689 | solution.py:52
  73.8 0.5 slice.25
  74.3 2.6 bitcast_dynamic-update-slice_fusion.2
  77.0 0.5 slice.25
  77.6 2.6 bitcast_dynamic-update-slice_fusion.2
  80.3 0.5 slice.25
  80.8 2.6 bitcast_dynamic-update-slice_fusion.2
  83.5 0.5 slice.25
  84.0 2.6 bitcast_dynamic-update-slice_fusion.2
  86.7 0.5 slice.25
  87.2 2.6 bitcast_dynamic-update-slice_fusion.2
  89.9 0.5 slice.25
  90.4 2.6 bitcast_dynamic-update-slice_fusion.2
  93.1 0.5 slice.25
  93.6 2.6 bitcast_dynamic-update-slice_fusion.2
  96.3 0.5 slice.25
  96.8 2.6 bitcast_dynamic-update-slice_fusion.2
  99.5 0.5 slice.25
  100.0 2.6 bitcast_dynamic-update-slice_fusion.2
  102.7 0.5 slice.25
  103.3 2.6 bitcast_dynamic-update-slice_fusion.2
  106.0 0.5 slice.25
  106.5 2.6 bitcast_dynamic-update-slice_fusion.2
  109.2 0.5 slice.25
  109.7 2.6 bitcast_dynamic-update-slice_fusion.2
  112.4 0.5 slice.25
  112.9 2.6 bitcast_dynamic-update-slice_fusion.2
  115.6 0.5 slice.25
  116.1 2.7 bitcast_dynamic-update-slice_fusion.2
  118.8 0.5 slice.25
  119.4 2.7 bitcast_dynamic-update-slice_fusion.2
  122.1 0.5 slice.25
  122.6 2.7 bitcast_dynamic-update-slice_fusion.2
  125.3 1.6 constant_dynamic-slice_fusion.1
  126.9 0.6 broadcast_in_dim.64
  127.5 6.7 %all-to-all-start.1 = ((s32[16,1,4]{2,1,0:T(1,128)}), s32[16,1,4]{2,1,0:T(1,128)S(1)}, u32[]{:S(2)}, u32[]{:S(2)}) async-start(s32[16,1,4]{2,1,0:T(1,128)} %broadcast_in_dim.64), calls=%async_computation.1 | async-start | bytes 16384 | tf_op jit(solution)/shard_map/all_to_all | solution.py:75
  134.2 7.0 %negate_bitcast_fusion = f32[16,2,4,128,128]{3,4,1,0,2:T(8,128)S(1)} fusion(bf16[4,128,1024,1,1]{2,1,4,3,0:T(8,128)(2,1)S(1)} %bitcast.66, bf16[16,2,128,1024,1]{3,2,1,0,4:T(8,128)(2,1)} %bitcast.67), kind=kOutput, calls=%fused_computation.5 | convolution fusion | flops 4297064448 | bytes 17825792 | tf_op jit(solution)/shard_map/ikap,jbp->ikjab/dot_general | solution.py:69
  141.2 3.8 copy.40
  145.0 7.0 %all-to-all-start.2 = ((f32[16,2,4,128,128]{3,4,1,2,0:T(8,128)}), f32[16,2,4,128,128]{3,4,1,2,0:T(8,128)}, u32[]{:S(2)}, u32[]{:S(2)}) async-start(f32[16,2,4,128,128]{3,4,1,2,0:T(8,128)} %copy.40), calls=%async_computation.2 | async-start | bytes 16777216 | tf_op jit(solution)/shard_map/all_to_all | solution.py:73
  152.0 0.2 all-reduce.4.cloned.1.call-start
  152.2 2.9 reshape.279
  155.1 3.5 copy.42
  159.4 115.5 %all-to-all-done.2 = f32[16,2,4,128,128]{3,4,1,2,0:T(8,128)} async-done(((f32[16,2,4,128,128]{3,4,1,2,0:T(8,128)}), f32[16,2,4,128,128]{3,4,1,2,0:T(8,128)}, u32[]{:S(2)}, u32[]{:S(2)}) %all-to-all-start.2) | async-done | bytes 8388640 | tf_op jit(solution)/shard_map/all_to_all | solution.py:73
  274.9 9.2 %copy.41 = f32[16,2,4,128,128]{4,3,2,1,0:T(8,128)} copy(f32[16,2,4,128,128]{3,4,1,2,0:T(8,128)} %all-to-all-done.2) | data formatting | bytes 16777216 | tf_op jit(solution)/shard_map/all_to_all | solution.py:73
  284.1 19.2 %scatter_fusion = f32[5,128,10,128]{3,1,2,0:T(8,128)S(1)} fusion(f32[5,128,10,128]{3,1,2,0:T(8,128)S(1)} %copy.42, s32[128]{0:T(128)S(1)} %reshape.318, f32[128,128,128]{2,1,0:T(8,128)} %bitcast.62), kind=kCustom, calls=%fused_computation.2 | custom fusion | flops 2097152 | bytes 25166848 | tf_op jit(solution)/shard_map/scatter-add | solution.py:78
  303.4 2.0 copy.43
  305.3 1.6 copy.47
  306.9 1.7 copy-done.3
  308.6 1.6 convolution_select_fusion
  310.3 59.8 %all-reduce.4.cloned.1.call-done = f32[640,256]{1,0:T(8,128)} async-done(((f32[640,256]{1,0:T(8,128)}), f32[640,256]{1,0:T(8,128)}) %all-reduce.4.cloned.1.call-update) | async-done | bytes 655376 | tf_op jit(solution)/shard_map/psum | solution.py:13
  370.1 83.8 %all-gather.5.cloned.1.call-done = f32[10240,256]{1,0:T(8,128)} async-done(((f32[640,256]{1,0:T(8,128)}), f32[10240,256]{1,0:T(8,128)}) %all-gather.5.cloned.1.call-update) | async-done | bytes 10485776 | tf_op jit(solution)/shard_map/all_gather | solution.py:86
  453.8 7.0 %convolution_subtract_fusion = f32[640,1280]{1,0:T(8,128)} fusion(f32[640,1280]{1,0:T(8,128)} %bitcast.65, f32[640,256]{1,0:T(8,128)} %all-reduce.4.cloned.1.call-done, f32[10240,256]{1,0:T(8,128)} %all-gather.5.cloned.1.call-done, s32[]{:T(128)S(6)} %select_n.153), kind=kOutput, calls=%fused_computation.6 | convolution fusion | flops 2517401600 | bytes 8519684 | tf_op jit(solution)/shard_map/dot_general | solution.py:88
  460.9 0.8 copy.58
  (59 shorter events, 2.5 us)
Async XLA Ops:
  7.2 1.6 copy-start
  7.2 5.7 %copy-start.2 = (s32[1,32]{1,0:T(1,128)S(1)}, s32[1,32]{1,0:T(1,128)}, u32[]{:S(2)}) copy-start(s32[1,32]{1,0:T(1,128)} %param.8) | copy-start | bytes 388
  7.2 58.5 %all-gather.3.cloned.1.call-start = ((), (), s32[]{:S(2)}) async-start(), calls=%async_computation.3 | async-start | bytes 9437184 | tf_op jit(solution)/shard_map/all_gather | solution.py:37
  14.7 112.2 %all-to-all-start = ((s32[16,1,2]{2,1,0:T(1,128)}), s32[16,1,2]{2,1,0:T(1,128)S(1)}, u32[]{:S(2)}, u32[]{:S(2)}) async-start(s32[16,1,2]{2,1,0:T(1,128)} %bitcast.3), calls=%async_computation | async-start | bytes 16384 | tf_op jit(solution)/shard_map/all_to_all | solution.py:74
  127.5 17.5 %all-to-all-start.1 = ((s32[16,1,4]{2,1,0:T(1,128)}), s32[16,1,4]{2,1,0:T(1,128)S(1)}, u32[]{:S(2)}, u32[]{:S(2)}) async-start(s32[16,1,4]{2,1,0:T(1,128)} %broadcast_in_dim.64), calls=%async_computation.1 | async-start | bytes 16384 | tf_op jit(solution)/shard_map/all_to_all | solution.py:75
  145.0 7.2 %copy-start.5 = (f32[640,1280]{1,0:T(8,128)S(1)}, f32[640,1280]{1,0:T(8,128)}, u32[]{:S(2)}) copy-start(f32[640,1280]{1,0:T(8,128)} %param.10) | copy-start | bytes 9830404
  145.0 129.9 %all-to-all-start.2 = ((f32[16,2,4,128,128]{3,4,1,2,0:T(8,128)}), f32[16,2,4,128,128]{3,4,1,2,0:T(8,128)}, u32[]{:S(2)}, u32[]{:S(2)}) async-start(f32[16,2,4,128,128]{3,4,1,2,0:T(8,128)} %copy.40), calls=%async_computation.2 | async-start | bytes 16777216 | tf_op jit(solution)/shard_map/all_to_all | solution.py:73
  152.0 218.1 %all-reduce.4.cloned.1.call-start = ((), (), s32[]{:S(2)}) async-start(), calls=%async_computation.4 | async-start | bytes 1310720 | tf_op jit(solution)/shard_map/psum | solution.py:13
  303.3 5.3 %copy-start.6 = (f32[256,256]{1,0:T(8,128)S(1)}, f32[256,256]{1,0:T(8,128)}, u32[]{:S(2)}) copy-start(f32[256,256]{1,0:T(8,128)} %param.11) | copy-start | bytes 786436
  305.3 156.4 %copy-start.1 = (bf16[1,1024,1024]{2,1,0:T(8,128)(2,1)S(1)}, bf16[1,1024,1024]{2,1,0:T(8,128)(2,1)}, u32[]{:S(2)}) copy-start(bf16[1,1024,1024]{2,1,0:T(8,128)(2,1)} %param.7) | copy-start | bytes 6291460
  306.9 1.7 copy-start.3
  310.2 143.6 %all-gather.5.cloned.1.call-start = ((), (), s32[]{:S(2)}) async-start(), calls=%async_computation.5 | async-start | bytes 11141120 | tf_op jit(solution)/shard_map/all_gather | solution.py:86
  370.0 90.9 %copy-start.4 = (f32[640,256]{1,0:T(8,128)S(1)}, f32[640,256]{1,0:T(8,128)}, u32[]{:S(2)}) copy-start(f32[640,256]{1,0:T(8,128)} %all-reduce.4.cloned.1.call-done) | copy-start | bytes 1966084
Sparse Core Ops, SparseCore 0:
  12.4 53.2 all-gather.2
  310.4 59.6 all-reduce.3
  372.2 81.6 all-gather.4
where the time goes:
time: 470 us; the launch traced here: 468 us
  waiting for transfers between devices  298 us (63%)
  local copies, waits for them, and re-layouts  91 us (19%)
  other arithmetic  22.9 us (5%)
  starting transfers between devices  22.4 us (5%)
  matrix products  19.1 us (4%)
  between operations  15.3 us (3%)
    all_to_all x1, waiting for transfers between devices, shards(): lax.all_to_all(contribution, 'row', split_axis=0, concat_axis=0, tiled=True)  115 us
    all_gather x1, waiting for transfers between devices, shards(): whole_panel = lax.all_gather(panel_rows, 'row', axis=0, tiled=True)  83.8 us
    psum x1, waiting for transfers between devices, from_root(): return lax.psum(kept, axis)  59.8 us
    gather x48, local copies, waits for them, and re-layouts  51.5 us
    all_gather x1, waiting for transfers between devices, shards(): factor = lax.all_gather(factor_part, 'col', axis=0, tiled=True)  38.6 us
    scatter-add x1, other arithmetic, shards(): tiled.at[arrived_rows[:, :, None], :, arrived_cols[:, None, :], :]  19.2 us
  transfers between devices with their start and end apart: 6, of which 4 were waited for; matrix products, arithmetic and copies ran while one was open for 18% of the time, Pallas kernels for 0%

commit v1 on v0

--- a/solution.py
+++ b/solution.py
@@ -83,7 +83,9 @@
         assembled[:, :PANEL], panel_inverse, (((1,), (1,)), ((), ())), precision=precise
     )
     panel_rows = from_root(own_panel, "col", 0)
-    whole_panel = lax.all_gather(panel_rows, "row", axis=0, tiled=True)
+    whole_panel = jnp.concatenate(
+        lax.all_to_all(jnp.stack([panel_rows] * lax.axis_size("row")), "row", 0, 0), axis=0
+    )
     across = lax.dynamic_slice_in_dim(whole_panel, column * cols_dev, cols_dev, 0)
     trailing = assembled - lax.dot_general(
         panel_rows, across, (((1,), (1,)), ((), ())), precision=precise

time: 470 us -> 558 us (1.19); the launches traced: 468 us -> 547 us
  waiting for transfers between devices: 298 us -> 364 us
  starting transfers between devices: 22.4 us -> 29.1 us
  local copies, waits for them, and re-layouts: 91 us -> 97 us
    all_to_all x0 -> x1, waiting for transfers between devices: none -> 150 us  [shards(): lax.all_to_all(jnp.stack([panel_rows] * lax.axis_size('row')), 'row', 0, 0)]
    all_gather x1 -> x0, waiting for transfers between devices: 83.8 us -> none  [shards(): whole_panel = lax.all_gather(panel_rows, 'row', axis=0, tiled=True)]
    all_to_all x0 -> x1, starting transfers between devices: none -> 6.84 us  [shards(): lax.all_to_all(jnp.stack([panel_rows] * lax.axis_size('row')), 'row', 0, 0)]
    another operation x0 -> x1, local copies, waits for them, and re-layouts: none -> 5.92 us  [shards(): jnp.stack([panel_rows] * lax.axis_size('row'))]
  transfers between devices with their start and end apart: 6 -> 6, of which waited for: 4 -> 4; matrix products, arithmetic and copies ran while one was open for 18% -> 15% of each run, Pallas kernels for 0% -> 0%
where the time goes in v1:
time: 558 us; the launch traced here: 547 us
  waiting for transfers between devices  364 us (65%)
  local copies, waits for them, and re-layouts  97 us (17%)
  starting transfers between devices  29.1 us (5%)
  other arithmetic  22.9 us (4%)
  matrix products  18.1 us (3%)
  between operations  15.6 us (3%)
    all_to_all x1, waiting for transfers between devices, shards(): lax.all_to_all(jnp.stack([panel_rows] * lax.axis_size('row')), 'row', 0, 0)  150 us
    all_to_all x1, waiting for transfers between devices, shards(): lax.all_to_all(contribution, 'row', split_axis=0, concat_axis=0, tiled=True)  115 us
    psum x1, waiting for transfers between devices, from_root(): return lax.psum(kept, axis)  59.8 us
    gather x48, local copies, waits for them, and re-layouts  51.6 us
    all_gather x1, waiting for transfers between devices, shards(): factor = lax.all_gather(factor_part, 'col', axis=0, tiled=True)  38.5 us
    scatter-add x1, other arithmetic, shards(): tiled.at[arrived_rows[:, :, None], :, arrived_cols[:, None, :], :]  19.2 us
  transfers between devices with their start and end apart: 6, of which 4 were waited for; matrix products, arithmetic and copies ran while one was open for 15% of the time, Pallas kernels for 0%

profile of v1, /device:TPU:1, one launch (start us, length us, event | category | flops | bytes accessed | tf_op | source)
XLA Modules:
  0.0 546.7 jit_solution(12028400441433557684)
XLA Ops:
  7.2 1.5 copy-done
  8.8 3.5 fusion.2
  13.2 0.7 gather_fusion
  14.0 0.7 subtract_select_fusion
  14.7 8.4 %all-to-all-start = ((s32[16,1,2]{2,1,0:T(1,128)}), s32[16,1,2]{2,1,0:T(1,128)S(1)}, u32[]{:S(2)}, u32[]{:S(2)}) async-start(s32[16,1,2]{2,1,0:T(1,128)} %bitcast.3), calls=%async_computation | async-start | bytes 16384 | tf_op jit(solution)/shard_map/all_to_all | solution.py:74
  23.2 0.7 fusion.12
  23.9 0.7 fusion.14
  24.6 0.6 gather_fusion.1
  26.0 1.2 compare_select_fusion.7
  27.2 38.5 %all-gather.2.cloned.1.call-done = bf16[4096,1024]{1,0:T(8,128)(2,1)} async-done(((bf16[512,1024]{1,0:T(8,128)(2,1)}), bf16[4096,1024]{1,0:T(8,128)(2,1)}) %all-gather.2.cloned.1.call-update) | async-done | bytes 8388624 | tf_op jit(solution)/shard_map/all_gather | solution.py:37
  65.7 8.0 %concatenate.10 = bf16[4608,1024]{1,0:T(8,128)(2,1)} pad(bf16[4096,1024]{1,0:T(8,128)(2,1)} %all-gather.2.cloned.1.call-done, bf16[]{:T(256)} %constant.41.clone.1), padding=0_512x0_0 | pad | bytes 17825794 | tf_op jit(solution)/shard_map/concatenate | solution.py:47
  73.7 51.6 %while.1 = (s32[]{:T(128)}, bf16[4608,1024]{1,0:T(8,128)(2,1)}, s32[16,2]{0,1:T(2,128)S(1)}, bf16[16,256,1024]{2,1,0:T(8,128)(2,1)}, s32[]{:T(128)}) while((s32[]{:T(128)}, bf16[4608,1024]{1,0:T(8,128)(2,1)}, s32[16,2]{0,1:T(2,128)S(1)}, bf16[16,256,1024]{2,1,0:T(8,128)(2,1)}, s32[]{:T(128)}) %tuple.22), condition=%wide.while_cond, body=%wide.while_body.sunk | while | flops 2 | bytes 1049689 | solution.py:52
  73.8 0.5 slice.25
  74.3 2.6 bitcast_dynamic-update-slice_fusion.2
  77.0 0.5 slice.25
  77.6 2.6 bitcast_dynamic-update-slice_fusion.2
  80.3 0.5 slice.25
  80.8 2.6 bitcast_dynamic-update-slice_fusion.2
  83.5 0.5 slice.25
  84.0 2.6 bitcast_dynamic-update-slice_fusion.2
  86.7 0.5 slice.25
  87.2 2.6 bitcast_dynamic-update-slice_fusion.2
  89.9 0.5 slice.25
  90.4 2.6 bitcast_dynamic-update-slice_fusion.2
  93.1 0.5 slice.25
  93.6 2.6 bitcast_dynamic-update-slice_fusion.2
  96.3 0.5 slice.25
  96.8 2.6 bitcast_dynamic-update-slice_fusion.2
  99.5 0.5 slice.25
  100.1 2.6 bitcast_dynamic-update-slice_fusion.2
  102.8 0.5 slice.25
  103.3 2.6 bitcast_dynamic-update-slice_fusion.2
  106.0 0.5 slice.25
  106.5 2.6 bitcast_dynamic-update-slice_fusion.2
  109.2 0.5 slice.25
  109.7 2.6 bitcast_dynamic-update-slice_fusion.2
  112.4 0.5 slice.25
  113.0 2.6 bitcast_dynamic-update-slice_fusion.2
  115.6 0.5 slice.25
  116.2 2.7 bitcast_dynamic-update-slice_fusion.2
  118.9 0.5 slice.25
  119.4 2.7 bitcast_dynamic-update-slice_fusion.2
  122.7 2.7 bitcast_dynamic-update-slice_fusion.2
  125.3 1.6 constant_dynamic-slice_fusion.1
  127.0 0.6 broadcast_in_dim.64
  127.6 6.7 %all-to-all-start.1 = ((s32[16,1,4]{2,1,0:T(1,128)}), s32[16,1,4]{2,1,0:T(1,128)S(1)}, u32[]{:S(2)}, u32[]{:S(2)}) async-start(s32[16,1,4]{2,1,0:T(1,128)} %broadcast_in_dim.64), calls=%async_computation.1 | async-start | bytes 16384 | tf_op jit(solution)/shard_map/all_to_all | solution.py:75
  134.3 7.0 %negate_bitcast_fusion = f32[16,2,4,128,128]{3,4,1,0,2:T(8,128)S(1)} fusion(bf16[4,128,1024,1,1]{2,1,4,3,0:T(8,128)(2,1)S(1)} %bitcast.67, bf16[16,2,128,1024,1]{3,2,1,0,4:T(8,128)(2,1)} %bitcast.68), kind=kOutput, calls=%fused_computation.5 | convolution fusion | flops 4297064448 | bytes 17825792 | tf_op jit(solution)/shard_map/ikap,jbp->ikjab/dot_general | solution.py:69
  141.2 3.8 copy.40
  145.1 7.0 %all-to-all-start.2 = ((f32[16,2,4,128,128]{3,4,1,2,0:T(8,128)}), f32[16,2,4,128,128]{3,4,1,2,0:T(8,128)}, u32[]{:S(2)}, u32[]{:S(2)}) async-start(f32[16,2,4,128,128]{3,4,1,2,0:T(8,128)} %copy.40), calls=%async_computation.2 | async-start | bytes 16777216 | tf_op jit(solution)/shard_map/all_to_all | solution.py:73
  152.3 2.9 reshape.284
  155.2 3.5 copy.42
  159.5 115.5 %all-to-all-done.2 = f32[16,2,4,128,128]{3,4,1,2,0:T(8,128)} async-done(((f32[16,2,4,128,128]{3,4,1,2,0:T(8,128)}), f32[16,2,4,128,128]{3,4,1,2,0:T(8,128)}, u32[]{:S(2)}, u32[]{:S(2)}) %all-to-all-start.2) | async-done | bytes 8388640 | tf_op jit(solution)/shard_map/all_to_all | solution.py:73
  275.0 9.2 %copy.41 = f32[16,2,4,128,128]{4,3,2,1,0:T(8,128)} copy(f32[16,2,4,128,128]{3,4,1,2,0:T(8,128)} %all-to-all-done.2) | data formatting | bytes 16777216 | tf_op jit(solution)/shard_map/all_to_all | solution.py:73
  284.2 19.2 %scatter_fusion = f32[5,128,10,128]{3,1,2,0:T(8,128)S(1)} fusion(f32[5,128,10,128]{3,1,2,0:T(8,128)S(1)} %copy.42, s32[128]{0:T(128)S(1)} %reshape.324, f32[128,128,128]{2,1,0:T(8,128)} %bitcast.63), kind=kCustom, calls=%fused_computation.2 | custom fusion | flops 2097152 | bytes 25166848 | tf_op jit(solution)/shard_map/scatter-add | solution.py:78
  303.4 2.0 copy.43
  305.4 1.6 copy.47
  307.0 1.7 copy-done.3
  308.7 1.6 convolution_select_fusion
  310.3 59.8 %all-reduce.4.cloned.1.call-done = f32[640,256]{1,0:T(8,128)} async-done(((f32[640,256]{1,0:T(8,128)}), f32[640,256]{1,0:T(8,128)}) %all-reduce.4.cloned.1.call-update) | async-done | bytes 655376 | tf_op jit(solution)/shard_map/psum | solution.py:13
  370.1 5.9 %stack.2 = f32[16,640,256]{2,1,0:T(8,128)} broadcast(f32[640,256]{1,0:T(8,128)} %all-reduce.4.cloned.1.call-done), dimensions={1,2} | broadcast | bytes 11141120 | tf_op jit(solution)/shard_map/stack | solution.py:87
  376.0 6.8 %all-to-all-start.3 = ((f32[16,640,256]{2,1,0:T(8,128)}), f32[16,640,256]{2,1,0:T(8,128)}, u32[]{:S(2)}, u32[]{:S(2)}) async-start(f32[16,640,256]{2,1,0:T(8,128)} %stack.2), calls=%async_computation.3 | async-start | bytes 20971520 | tf_op jit(solution)/shard_map/all_to_all | solution.py:87
  382.9 150.1 %all-to-all-done.3 = f32[16,640,256]{2,1,0:T(8,128)} async-done(((f32[16,640,256]{2,1,0:T(8,128)}), f32[16,640,256]{2,1,0:T(8,128)}, u32[]{:S(2)}, u32[]{:S(2)}) %all-to-all-start.3) | async-done | bytes 10485792 | tf_op jit(solution)/shard_map/all_to_all | solution.py:87
  532.9 6.0 %convolution_subtract_fusion = f32[640,1280]{1,0:T(8,128)} fusion(f32[640,1280]{1,0:T(8,128)} %bitcast.66, f32[640,256]{1,0:T(8,128)S(1)} %copy-done.4, f32[10240,256]{1,0:T(8,128)} %bitcast.17, s32[]{:T(128)S(6)} %select_n.153), kind=kOutput, calls=%fused_computation.6 | convolution fusion | flops 2517401600 | bytes 8519684 | tf_op jit(solution)/shard_map/dot_general | solution.py:90
  539.0 0.8 copy.58
  (59 shorter events, 3.2 us)
Async XLA Ops:
  7.2 1.6 copy-start
  7.2 5.7 %copy-start.2 = (s32[1,32]{1,0:T(1,128)S(1)}, s32[1,32]{1,0:T(1,128)}, u32[]{:S(2)}) copy-start(s32[1,32]{1,0:T(1,128)} %param.8) | copy-start | bytes 388
  7.2 58.5 %all-gather.2.cloned.1.call-start = ((), (), s32[]{:S(2)}) async-start(), calls=%async_computation.4 | async-start | bytes 9437184 | tf_op jit(solution)/shard_map/all_gather | solution.py:37
  14.7 112.3 %all-to-all-start = ((s32[16,1,2]{2,1,0:T(1,128)}), s32[16,1,2]{2,1,0:T(1,128)S(1)}, u32[]{:S(2)}, u32[]{:S(2)}) async-start(s32[16,1,2]{2,1,0:T(1,128)} %bitcast.3), calls=%async_computation | async-start | bytes 16384 | tf_op jit(solution)/shard_map/all_to_all | solution.py:74
  127.6 17.5 %all-to-all-start.1 = ((s32[16,1,4]{2,1,0:T(1,128)}), s32[16,1,4]{2,1,0:T(1,128)S(1)}, u32[]{:S(2)}, u32[]{:S(2)}) async-start(s32[16,1,4]{2,1,0:T(1,128)} %broadcast_in_dim.64), calls=%async_computation.1 | async-start | bytes 16384 | tf_op jit(solution)/shard_map/all_to_all | solution.py:75
  145.1 7.2 %copy-start.5 = (f32[640,1280]{1,0:T(8,128)S(1)}, f32[640,1280]{1,0:T(8,128)}, u32[]{:S(2)}) copy-start(f32[640,1280]{1,0:T(8,128)} %param.10) | copy-start | bytes 9830404
  145.1 129.9 %all-to-all-start.2 = ((f32[16,2,4,128,128]{3,4,1,2,0:T(8,128)}), f32[16,2,4,128,128]{3,4,1,2,0:T(8,128)}, u32[]{:S(2)}, u32[]{:S(2)}) async-start(f32[16,2,4,128,128]{3,4,1,2,0:T(8,128)} %copy.40), calls=%async_computation.2 | async-start | bytes 16777216 | tf_op jit(solution)/shard_map/all_to_all | solution.py:73
  152.0 218.0 %all-reduce.4.cloned.1.call-start = ((), (), s32[]{:S(2)}) async-start(), calls=%async_computation.5 | async-start | bytes 1310720 | tf_op jit(solution)/shard_map/psum | solution.py:13
  303.4 5.3 copy-start.6
  307.0 1.7 copy-start.3
  376.0 156.9 %copy-start.4 = (f32[640,256]{1,0:T(8,128)S(1)}, f32[640,256]{1,0:T(8,128)}, u32[]{:S(2)}) copy-start(f32[640,256]{1,0:T(8,128)} %all-reduce.4.cloned.1.call-done) | copy-start | bytes 1966084
  376.0 156.9 %all-to-all-start.3 = ((f32[16,640,256]{2,1,0:T(8,128)}), f32[16,640,256]{2,1,0:T(8,128)}, u32[]{:S(2)}, u32[]{:S(2)}) async-start(f32[16,640,256]{2,1,0:T(8,128)} %stack.2), calls=%async_computation.3 | async-start | bytes 20971520 | tf_op jit(solution)/shard_map/all_to_all | solution.py:87
  382.9 157.0 %copy-start.1 = (bf16[1,1024,1024]{2,1,0:T(8,128)(2,1)S(1)}, bf16[1,1024,1024]{2,1,0:T(8,128)(2,1)}, u32[]{:S(2)}) copy-start(bf16[1,1024,1024]{2,1,0:T(8,128)(2,1)} %param.7) | copy-start | bytes 6291460
Sparse Core Ops, SparseCore 0:
  12.4 53.2 all-gather.1
  310.4 59.6 all-reduce.3
